TPU v7x, 32 devices: a whole 2x2x4 slice. The times are simulated.
32 devices in a mesh: row: 4 (over y, core), col: 8 (over z, x).
Axes of the slice: x: 2, y: 2, z: 4, core: 2. Of those that a mesh axis runs over, the one named last changes fastest.
Arguments:
- ancestor_inverse: float32 [12288, 12288], P('row', 'col')
- factor: bfloat16 [3, 12288, 512], P(None, ('row', 'col')), may hold values from -0.5 to 0.5
- coupling: float32 [3, 512, 512], replicated, may hold values from -0.25 to 0.25
- diagonal_inverse: float32 [3, 512, 512], replicated, may hold values from -6 to 6
- ancestors: int32 [3, 24], replicated, may hold values from -1 to 23, as said below
Outputs:
- block_columns: float32 [3, 12288, 512], P(None, ('row', 'col'))
- block_rows: float32 [3, 12288, 512], P(None, ('col', 'row'))
- node_blocks: float32 [3, 3, 512, 512], replicated
Inputs may be any that keep to these rules, and one draw needn't show every extreme that they name: `ancestors`: row k lists the ancestor block rows of supernode k, blocks of 512 rows: distinct indices in increasing order, then -1 in the slots left. Every block is listed by some supernode.
All inputs are finite; a program needn't handle non-finite values.
Results may differ from a plain program's by a relative error of at most 0.0003.
Values may be sent and summed in bfloat16 or wider, within the bound.
No kernel may reach another device: no remote copies, remote signals or barrier semaphores. Data moves between devices by JAX's collectives and lax.ppermute only.
A program may use at most 128 MiB of HBM per device.

v0:
```python
import jax
import jax.numpy as jnp
from jax import lax
from jax.sharding import PartitionSpec as P

highest = lax.Precision.HIGHEST


def broadcast(value, axis, source):
    kept = jnp.where(lax.axis_index(axis) == source, value, 0).astype(value.dtype)
    return lax.psum(kept, axis)


def matmul(left, right):
    return jnp.dot(left, right, precision=highest)


def left_dot(left, right):
    return lax.dot_general(left, right, (((0,), (0,)), ((), ())), precision=highest)


def pair_index(later, earlier):
    return later * (later - 1) // 2 + earlier


def local(ancestor_inverse, factor, coupling, diagonal_inverse, ancestors):
    col_count = lax.axis_size("col")
    row_index = lax.axis_index("row")
    col_index = lax.axis_index("col")
    nodes_total, piece_rows, sn_width = factor.shape
    rows_here, cols_here = ancestor_inverse.shape
    group_ratio = rows_here // cols_here
    first_row = (row_index * col_count + col_index) * piece_rows
    block_of_row = (first_row + jnp.arange(piece_rows, dtype=jnp.int32)) // sn_width
    source_row = col_index // group_ratio
    block_start = col_index % group_ratio * cols_here
    row_layout = []
    col_layout = []
    solved = {}
    for current in range(nodes_total):
        listed = jnp.any(ancestors[current][:, None] == block_of_row[None, :], axis=0)
        lower_part = jnp.where(listed[:, None], factor[current], jnp.zeros_like(factor[current]))
        lower_rows = lax.all_gather(lower_part, "col", axis=0, tiled=True)
        own_block = lax.dynamic_slice_in_dim(lower_rows, block_start, cols_here, 0)
        lower_cols = broadcast(own_block, "row", source_row).astype(jnp.float32)
        lower_here = lower_part.astype(jnp.float32)
        product_sum = lax.psum_scatter(
            matmul(ancestor_inverse, lower_cols), "col", scatter_dimension=0, tiled=True
        )
        for earlier in range(current):
            product_sum = product_sum + matmul(
                row_layout[earlier], coupling[pair_index(current, earlier)]
            )
        column = -product_sum
        stacked = jnp.concatenate(row_layout + [column], axis=1)
        summed = lax.psum(left_dot(lower_here, stacked), ("row", "col"))
        crosses = [
            summed[:, earlier * sn_width : (earlier + 1) * sn_width] for earlier in range(current)
        ]
        self_term = summed[:, current * sn_width : (current + 1) * sn_width]
        for earlier in range(current):
            block_value = -crosses[earlier].T
            for inner in range(current):
                block_value = block_value - matmul(
                    solved[earlier, inner], coupling[pair_index(current, inner)]
                )
            solved[earlier, current] = block_value
            solved[current, earlier] = block_value.T
        diag_value = diagonal_inverse[current] - self_term
        for earlier in range(current):
            diag_value = diag_value - left_dot(
                coupling[pair_index(current, earlier)], solved[earlier, current]
            )
        solved[current, current] = diag_value
        rows_float = lower_rows.astype(jnp.float32)
        mirror = lax.psum_scatter(
            left_dot(ancestor_inverse, rows_float), "row", scatter_dimension=0, tiled=True
        )
        for earlier in range(current):
            mirror = mirror + matmul(col_layout[earlier], coupling[pair_index(current, earlier)])
        col_layout.append(-mirror)
        row_layout.append(column)
    finished = jnp.stack(row_layout)
    mirrored_all = jnp.stack(col_layout)
    node_blocks = jnp.stack(
        [
            jnp.stack([solved[first_node, second_node] for second_node in range(nodes_total)])
            for first_node in range(nodes_total)
        ]
    )
    return (finished, mirrored_all, node_blocks)


def solution(mesh):
    placed = (P("row", "col"), P(None, ("row", "col"), None), P(), P(), P())
    return jax.shard_map(
        local,
        mesh=mesh,
        in_specs=placed,
        out_specs=(P(None, ("row", "col"), None), P(None, ("col", "row"), None), P()),
        check_vma=False,
    )
```

profile of v0, /device:TPU:0, one launch (start us, length us, event | category | flops | bytes accessed | tf_op | source)
XLA Modules:
  0.0 1007.5 jit_solution(5974017174490358877)
XLA Ops:
  7.2 0.8 slice_bitcast_fusion.2
  8.1 2.5 bitcast_select_fusion.1
  10.7 0.7 all-gather.4.cloned.1.call-update
  11.5 0.7 all-gather.6.cloned.1.call-update
  12.2 61.3 %all-gather.8.cloned.1.call-done = bf16[3072,512]{1,0:T(8,128)(2,1)} async-done(((bf16[384,512]{1,0:T(8,128)(2,1)}), bf16[3072,512]{1,0:T(8,128)(2,1)}) %all-gather.8.cloned.1.call-update) | async-done | bytes 3145744 | tf_op jit(solution)/shard_map/all_gather | solution.py:43
  73.6 2.8 dynamic-slice_select_fusion
  76.4 58.1 %all-gather.4.cloned.1.call-done = bf16[3072,512]{1,0:T(8,128)(2,1)} async-done(((bf16[384,512]{1,0:T(8,128)(2,1)}), bf16[3072,512]{1,0:T(8,128)(2,1)}) %all-gather.4.cloned.1.call-update) | async-done | bytes 3145744 | tf_op jit(solution)/shard_map/all_gather | solution.py:43
  134.5 2.8 dynamic-slice_select_fusion.2
  137.3 58.1 %all-gather.6.cloned.1.call-done = bf16[3072,512]{1,0:T(8,128)(2,1)} async-done(((bf16[384,512]{1,0:T(8,128)(2,1)}), bf16[3072,512]{1,0:T(8,128)(2,1)}) %all-gather.6.cloned.1.call-update) | async-done | bytes 3145744 | tf_op jit(solution)/shard_map/all_gather | solution.py:43
  195.4 2.8 dynamic-slice_select_fusion.1
  198.3 92.8 %all-reduce.7.cloned.1.call-done = (bf16[1536,512]{1,0:T(8,128)(2,1)}, bf16[1536,512]{1,0:T(8,128)(2,1)}, bf16[1536,512]{1,0:T(8,128)(2,1)}) async-done(((bf16[1536,512]{1,0:T(8,128)(2,1)}, bf16[1536,512]{1,0:T(8,128)(2,1)}, bf16[1536,512]{1,0:T(8,128)(2,1)}), (bf16[1536,512]{1,0:T(8,128)(2,1)}, bf16[1536,512]{1,0:T(8,128)(2,1)}, bf16[1536,512]{1,0:T(8,128)(2,1)})) %all-reduce.7.cloned.1.call-update) | async-done | bytes 4718608 | tf_op jit(solution)/shard_map/psum | solution.py:11
  291.1 22.4 %convolution_bitcast_fusion.2 = f32[3072,512]{0,1:T(8,128)} fusion(bf16[1536,512]{1,0:T(8,128)(2,1)} %get-tuple-element.16, f32[3072,1536]{1,0:T(8,128)} %param.5), kind=kOutput, calls=%fused_computation.3 | convolution fusion | flops 28991029248 | bytes 26738688 | tf_op jit(solution)/shard_map/dot_general | solution.py:15
  313.5 1.3 copy-done.30
  314.9 21.8 %convolution_bitcast_fusion.1 = f32[3072,512]{0,1:T(8,128)} fusion(bf16[1536,512]{1,0:T(8,128)(2,1)S(1)} %copy-done.30, f32[3072,1536]{1,0:T(8,128)} %param.5), kind=kOutput, calls=%fused_computation.2 | convolution fusion | flops 28991029248 | bytes 26738688 | tf_op jit(solution)/shard_map/dot_general | solution.py:15
  336.7 0.5 reduce-scatter.11.cloned.1.call-start
  337.2 0.9 copy-done.29
  338.1 21.8 %convolution_bitcast_fusion = f32[3072,512]{0,1:T(8,128)} fusion(bf16[1536,512]{1,0:T(8,128)(2,1)S(1)} %copy-done.29, f32[3072,1536]{1,0:T(8,128)} %param.5), kind=kOutput, calls=%fused_computation.1 | convolution fusion | flops 28991029248 | bytes 26738688 | tf_op jit(solution)/shard_map/dot_general | solution.py:15
  360.0 1.9 copy-done.28
  361.8 19.7 %convolution_bitcast_fusion.3 = f32[1536,512]{0,1:T(8,128)} fusion(bf16[3072,512]{1,0:T(8,128)(2,1)S(1)} %copy-done.28, f32[3072,1536]{1,0:T(8,128)} %param.5), kind=kOutput, calls=%fused_computation.4 | convolution fusion | flops 28991029248 | bytes 25165824 | tf_op jit(solution)/shard_map/dot_general | solution.py:19
  381.8 1.7 copy-done.27
  383.5 19.9 %convolution_bitcast_fusion.5 = f32[1536,512]{0,1:T(8,128)} fusion(bf16[3072,512]{1,0:T(8,128)(2,1)S(1)} %copy-done.27, f32[3072,1536]{1,0:T(8,128)} %param.5), kind=kOutput, calls=%fused_computation.6 | convolution fusion | flops 28991029248 | bytes 25165824 | tf_op jit(solution)/shard_map/dot_general | solution.py:19
  403.5 1.8 copy-done.26
  405.3 19.7 %convolution_bitcast_fusion.4 = f32[1536,512]{0,1:T(8,128)} fusion(bf16[3072,512]{1,0:T(8,128)(2,1)S(1)} %copy-done.26, f32[3072,1536]{1,0:T(8,128)} %param.5), kind=kOutput, calls=%fused_computation.5 | convolution fusion | flops 28991029248 | bytes 25165824 | tf_op jit(solution)/shard_map/dot_general | solution.py:19
  425.3 6.5 reduce-scatter.7.cloned.1.call-done
  431.8 2.4 fusion.73
  434.2 3.3 fusion.64
  437.5 115.1 %reduce-scatter.9.cloned.1.call-done = f32[384,512]{0,1:T(8,128)} async-done(((f32[3072,512]{0,1:T(8,128)}), f32[384,512]{0,1:T(8,128)}) %reduce-scatter.9.cloned.1.call-update) | async-done | bytes 786448 | tf_op jit(solution)/shard_map/reduce_scatter | solution.py:47
  552.6 3.4 fusion.14
  555.9 0.9 copy-done.3
  556.9 3.1 fusion.6
  560.0 114.0 %reduce-scatter.11.cloned.1.call-done = f32[384,512]{0,1:T(8,128)} async-done(((f32[3072,512]{0,1:T(8,128)}), f32[384,512]{0,1:T(8,128)}) %reduce-scatter.11.cloned.1.call-update) | async-done | bytes 786448 | tf_op jit(solution)/shard_map/reduce_scatter | solution.py:47
  674.0 3.3 convolution_add_fusion.4
  677.4 1.9 fusion.15
  679.3 0.9 copy-done.12
  680.2 4.5 fusion
  684.7 2.3 slice.74
  687.0 2.9 copy.65
  690.0 23.6 %reduce-scatter.17.cloned.1.call-done = f32[384,512]{0,1:T(8,128)} async-done(((f32[1536,512]{0,1:T(8,128)}), f32[384,512]{0,1:T(8,128)}) %reduce-scatter.17.cloned.1.call-update) | async-done | bytes 786448 | tf_op jit(solution)/shard_map/reduce_scatter | solution.py:76
  713.6 40.3 %reduce-scatter.13.cloned.1.call-done = f32[384,512]{0,1:T(8,128)} async-done(((f32[1536,512]{0,1:T(8,128)}), f32[384,512]{0,1:T(8,128)}) %reduce-scatter.13.cloned.1.call-update) | async-done | bytes 786448 | tf_op jit(solution)/shard_map/reduce_scatter | solution.py:76
  753.9 4.1 convolution_add_fusion.1
  758.0 36.0 %reduce-scatter.15.cloned.1.call-done = f32[384,512]{0,1:T(8,128)} async-done(((f32[1536,512]{0,1:T(8,128)}), f32[384,512]{0,1:T(8,128)}) %reduce-scatter.15.cloned.1.call-update) | async-done | bytes 786448 | tf_op jit(solution)/shard_map/reduce_scatter | solution.py:76
  794.0 3.4 fusion.16
  797.4 1.9 fusion.18
  799.4 1.6 pad_maximum_fusion.2
  800.9 3.0 copy.51
  804.0 3.2 pad_maximum_fusion.1
  807.1 3.2 copy.50
  810.3 146.5 %all-reduce.5.cloned.1.call-done = (f32[512,1536]{1,0:T(8,128)}, f32[512,512]{1,0:T(8,128)}, f32[512,1024]{0,1:T(8,128)}) async-done(((f32[512,1536]{1,0:T(8,128)}, f32[512,512]{1,0:T(8,128)}, f32[512,1024]{0,1:T(8,128)}), (f32[512,1536]{1,0:T(8,128)}, f32[512,512]{1,0:T(8,128)}, f32[512,1024]{0,1:T(8,128)})) %all-reduce.5.cloned.1.call-update) | async-done | bytes 6291472 | tf_op jit(solution)/shard_map/psum | solution.py:56
  956.9 3.6 fusion.34
  960.5 3.2 bitcast_subtract_fusion.7
  963.7 1.9 fusion.32
  965.6 1.9 fusion.27
  967.5 2.0 fusion.13
  969.5 1.0 copy-done.8
  970.5 1.9 fusion.25
  972.4 3.3 fusion.12
  975.7 2.3 fusion.20
  978.0 2.3 fusion.70
  980.3 2.5 copy.39
  982.9 5.3 fusion.11
  988.2 2.0 maximum_bitcast_fusion.1
  990.1 2.4 copy.49
  992.6 2.3 maximum_bitcast_fusion.2
  995.6 5.1 pad_maximum_fusion
  (77 shorter events, 1.9 us)
Async XLA Ops:
  7.2 66.4 %all-gather.8.cloned.1.call-start = ((), (), s32[]{:S(2)}) async-start(), calls=%async_computation.10 | async-start | bytes 3538944 | tf_op jit(solution)/shard_map/all_gather | solution.py:43
  10.7 123.8 %all-gather.4.cloned.1.call-start = ((), (), s32[]{:S(2)}) async-start(), calls=%async_computation.6 | async-start | bytes 3538944 | tf_op jit(solution)/shard_map/all_gather | solution.py:43
  11.4 183.9 %all-gather.6.cloned.1.call-start = ((), (), s32[]{:S(2)}) async-start(), calls=%async_computation.8 | async-start | bytes 3538944 | tf_op jit(solution)/shard_map/all_gather | solution.py:43
  12.2 278.9 %all-reduce.7.cloned.1.call-start = ((), (), s32[]{:S(2)}) async-start(), calls=%async_computation.16 | async-start | bytes 9437184 | tf_op jit(solution)/shard_map/psum | solution.py:11
  198.2 233.6 %reduce-scatter.7.cloned.1.call-start = ((), (), s32[]{:S(2)}) async-start(), calls=%async_computation.7 | async-start | bytes 7077888 | tf_op jit(solution)/shard_map/reduce_scatter | solution.py:47
  313.5 1.4 copy-start.30
  313.5 239.1 %reduce-scatter.9.cloned.1.call-start = ((), (), s32[]{:S(2)}) async-start(), calls=%async_computation.9 | async-start | bytes 7077888 | tf_op jit(solution)/shard_map/reduce_scatter | solution.py:47
  336.7 1.4 copy-start.29
  336.7 337.3 %reduce-scatter.11.cloned.1.call-start = ((), (), s32[]{:S(2)}) async-start(), calls=%async_computation.11 | async-start | bytes 7077888 | tf_op jit(solution)/shard_map/reduce_scatter | solution.py:47
  359.9 1.9 copy-start.28
  359.9 353.6 %reduce-scatter.17.cloned.1.call-start = ((), (), s32[]{:S(2)}) async-start(), calls=%async_computation.14 | async-start | bytes 3932160 | tf_op jit(solution)/shard_map/reduce_scatter | solution.py:76
  381.6 2.0 copy-start.27
  381.6 372.2 %reduce-scatter.13.cloned.1.call-start = ((), (), s32[]{:S(2)}) async-start(), calls=%async_computation.12 | async-start | bytes 3932160 | tf_op jit(solution)/shard_map/reduce_scatter | solution.py:76
  403.4 1.9 copy-start.26
  403.5 390.5 %reduce-scatter.15.cloned.1.call-start = ((), (), s32[]{:S(2)}) async-start(), calls=%async_computation.13 | async-start | bytes 3932160 | tf_op jit(solution)/shard_map/reduce_scatter | solution.py:76
  425.0 9.2 copy-start.23
  425.0 127.6 %copy-start = (f32[3,512,512]{2,1,0:T(8,128)S(1)}, f32[3,512,512]{2,1,0:T(8,128)}, u32[]{:S(2)}) copy-start(f32[3,512,512]{2,1,0:T(8,128)} %param.7) | copy-start | bytes 9437188
  425.0 531.9 %all-reduce.5.cloned.1.call-start = ((), (), s32[]{:S(2)}) async-start(), calls=%async_computation.15 | async-start | bytes 12582912 | tf_op jit(solution)/shard_map/psum | solution.py:56
  437.5 119.4 %copy-start.24 = (bf16[384,512]{1,0:T(8,128)(2,1)S(1)}, bf16[384,512]{1,0:T(8,128)(2,1)}, u32[]{:S(2)}) copy-start(bf16[384,512]{1,0:T(8,128)(2,1)} %get-tuple-element.22) | copy-start | bytes 1179652
  552.6 4.3 copy-start.13
  555.9 0.9 copy-start.3
  560.0 120.2 %copy-start.16 = (bf16[384,512]{1,0:T(8,128)(2,1)S(1)}, bf16[384,512]{1,0:T(8,128)(2,1)}, u32[]{:S(2)}) copy-start(bf16[384,512]{1,0:T(8,128)(2,1)} %get-tuple-element.24) | copy-start | bytes 1179652
  674.0 3.4 copy-start.4
  674.0 6.2 copy-start.14
  679.2 0.9 copy-start.12
  794.0 3.4 copy-start.25
  794.0 5.3 copy-start.15
  956.9 3.6 copy-start.10
  956.9 3.6 copy-start.11
  963.7 3.8 copy-start.1
  963.7 3.8 copy-start.17
  963.7 3.8 copy-start.18
  965.6 12.4 %copy-start.5 = (f32[512,512]{0,1:T(8,128)}, f32[512,512]{0,1:T(8,128)S(1)}, u32[]{:S(2)}) copy-start(f32[512,512]{0,1:T(8,128)S(1)} %fusion.32) | copy-start | bytes 3145732
  967.5 4.9 copy-start.7
  969.5 1.0 copy-start.8
  972.4 5.6 copy-start.6
  982.9 5.3 copy-start.9
  982.9 5.3 copy-start.21
  982.9 5.3 copy-start.22
  992.5 2.4 copy-start.2
  992.5 2.5 copy-start.19
  992.5 2.8 copy-start.20
Sparse Core Ops, SparseCore 0:
  10.8 62.7 all-gather.7
  75.7 58.6 all-gather.3
  136.7 58.6 all-gather.5
  198.3 92.7 all-reduce.6
  313.6 118.1 reduce-scatter.6
  435.2 117.2 reduce-scatter.8
  556.7 117.2 reduce-scatter.10
  676.5 36.9 reduce-scatter.16
  716.1 37.7 reduce-scatter.12
  756.2 37.7 reduce-scatter.14
  800.5 156.3 all-reduce.4
where the time goes:
time: 1020 us; the launch traced here: 1010 us
  waiting for transfers between devices  754 us (74%)
  matrix products  177 us (17%)
  other arithmetic  32.6 us (3%)
  local copies, waits for them, and re-layouts  28.1 us (3%)
  between operations  14.5 us (1%)
    reduce_scatter x3, waiting for transfers between devices, local(): lax.psum_scatter(matmul(ancestor_inverse, lower_cols), 'col', scatter_dim...  236 us
    all_gather x3, waiting for transfers between devices, local(): lower_rows = lax.all_gather(lower_part, 'col', axis=0, tiled=True)  177 us
    psum x1, waiting for transfers between devices, local(): summed = lax.psum(left_dot(lower_here, stacked), ('row', 'col'))  147 us
    reduce_scatter x3, waiting for transfers between devices, local(): lax.psum_scatter(left_dot(ancestor_inverse, rows_float), 'row', scatter_d...  99.9 us
    dot_general x14, matrix products, matmul(): return jnp.dot(left, right, precision=highest)  96.3 us
    psum x1, waiting for transfers between devices, broadcast(): return lax.psum(kept, axis)  92.8 us
    dot_general x9, matrix products, left_dot(): lax.dot_general(left, right, (((0,), (0,)), ((), ())), precision=highest)  80.7 us
  transfers between devices with their start and end apart: 11, of which 11 were waited for; matrix products, arithmetic and copies ran while one was open for 15% of the time, Pallas kernels for 0%

commit v1 on v0

--- a/solution.py
+++ b/solution.py
@@ -53,7 +53,9 @@
             )
         column = -product_sum
         stacked = jnp.concatenate(row_layout + [column], axis=1)
-        summed = lax.psum(left_dot(lower_here, stacked), ("row", "col"))
+        summed = left_dot(lower_here, stacked)
+        for mesh_axis in ("row", "col"):
+            summed = lax.psum(summed, mesh_axis)
         crosses = [
             summed[:, earlier * sn_width : (earlier + 1) * sn_width] for earlier in range(current)
         ]

time: 1020 us -> 1200 us (1.18)
  waiting for transfers between devices: 754 us -> 937 us
    psum x1 -> x2, waiting for transfers between devices: 147 us -> 254 us  [local(): summed = lax.psum(summed, mesh_axis)]
    reduce_scatter x3, waiting for transfers between devices: 236 us -> 299 us  [local(): lax.psum_scatter(matmul(ancestor_inverse, lower_cols), 'col', scatter_dim...]
    reduce_scatter x3, waiting for transfers between devices: 99.9 us -> 113 us  [local(): lax.psum_scatter(left_dot(ancestor_inverse, rows_float), 'row', scatter_d...]
  transfers between devices with their start and end apart: 11 -> 12, of which waited for: 11 -> 12; matrix products, arithmetic and copies ran while one was open for 15% -> 12% of each run, Pallas kernels for 0% -> 0%
where the time goes in v1:
time: 1200 us
  waiting for transfers between devices  937 us (78%)
  matrix products  180 us (15%)
  other arithmetic  31.1 us (3%)
  local copies, waits for them, and re-layouts  19.7 us (2%)
  between operations  15 us (1%)
  starting transfers between devices  12.7 us (1%)
    reduce_scatter x3, waiting for transfers between devices, local(): lax.psum_scatter(matmul(ancestor_inverse, lower_cols), 'col', scatter_dim...  299 us
    psum x2, waiting for transfers between devices, local(): summed = lax.psum(summed, mesh_axis)  254 us
    all_gather x3, waiting for transfers between devices, local(): lower_rows = lax.all_gather(lower_part, 'col', axis=0, tiled=True)  177 us
    reduce_scatter x3, waiting for transfers between devices, local(): lax.psum_scatter(left_dot(ancestor_inverse, rows_float), 'row', scatter_d...  113 us
    dot_general x14, matrix products, matmul(): return jnp.dot(left, right, precision=highest)  97.1 us
    psum x1, waiting for transfers between devices, broadcast(): return lax.psum(kept, axis)  92.8 us
    dot_general x9, matrix products, left_dot(): lax.dot_general(left, right, (((0,), (0,)), ((), ())), precision=highest)  82.4 us
  transfers between devices with their start and end apart: 12, of which 12 were waited for; matrix products, arithmetic and copies ran while one was open for 12% of the time, Pallas kernels for 0%

profile of v1, /device:TPU:0, one launch (start us, length us, event | category | flops | bytes accessed | tf_op | source)
XLA Modules:
  0.0 1195.5 jit_solution(811163514902072832)
XLA Ops:
  7.2 0.8 slice_bitcast_fusion.2
  8.1 2.5 bitcast_select_fusion.1
  10.7 0.7 all-gather.4.cloned.1.call-update
  11.4 0.7 all-gather.6.cloned.1.call-update
  12.2 61.3 %all-gather.8.cloned.1.call-done = bf16[3072,512]{1,0:T(8,128)(2,1)} async-done(((bf16[384,512]{1,0:T(8,128)(2,1)}), bf16[3072,512]{1,0:T(8,128)(2,1)}) %all-gather.8.cloned.1.call-update) | async-done | bytes 3145744 | tf_op jit(solution)/shard_map/all_gather | solution.py:43
  73.5 2.8 dynamic-slice_select_fusion
  76.3 58.1 %all-gather.4.cloned.1.call-done = bf16[3072,512]{1,0:T(8,128)(2,1)} async-done(((bf16[384,512]{1,0:T(8,128)(2,1)}), bf16[3072,512]{1,0:T(8,128)(2,1)}) %all-gather.4.cloned.1.call-update) | async-done | bytes 3145744 | tf_op jit(solution)/shard_map/all_gather | solution.py:43
  134.4 2.8 dynamic-slice_select_fusion.2
  137.2 58.1 %all-gather.6.cloned.1.call-done = bf16[3072,512]{1,0:T(8,128)(2,1)} async-done(((bf16[384,512]{1,0:T(8,128)(2,1)}), bf16[3072,512]{1,0:T(8,128)(2,1)}) %all-gather.6.cloned.1.call-update) | async-done | bytes 3145744 | tf_op jit(solution)/shard_map/all_gather | solution.py:43
  195.3 2.8 dynamic-slice_select_fusion.1
  198.2 92.8 %all-reduce.11.cloned.1.call-done = (bf16[1536,512]{1,0:T(8,128)(2,1)}, bf16[1536,512]{1,0:T(8,128)(2,1)}, bf16[1536,512]{1,0:T(8,128)(2,1)}) async-done(((bf16[1536,512]{1,0:T(8,128)(2,1)}, bf16[1536,512]{1,0:T(8,128)(2,1)}, bf16[1536,512]{1,0:T(8,128)(2,1)}), (bf16[1536,512]{1,0:T(8,128)(2,1)}, bf16[1536,512]{1,0:T(8,128)(2,1)}, bf16[1536,512]{1,0:T(8,128)(2,1)})) %all-reduce.11.cloned.1.call-update) | async-done | bytes 4718608 | tf_op jit(solution)/shard_map/psum | solution.py:11
  291.0 22.2 %convolution_bitcast_fusion = f32[3072,512]{0,1:T(8,128)} fusion(bf16[1536,512]{1,0:T(8,128)(2,1)} %get-tuple-element.18, f32[3072,1536]{1,0:T(8,128)} %param.5), kind=kOutput, calls=%fused_computation.1 | convolution fusion | flops 28991029248 | bytes 26738688 | tf_op jit(solution)/shard_map/dot_general | solution.py:15
  313.4 1.3 copy-done.26
  314.7 21.8 %convolution_bitcast_fusion.2 = f32[3072,512]{0,1:T(8,128)} fusion(bf16[1536,512]{1,0:T(8,128)(2,1)S(1)} %copy-done.26, f32[3072,1536]{1,0:T(8,128)} %param.5), kind=kOutput, calls=%fused_computation.3 | convolution fusion | flops 28991029248 | bytes 26738688 | tf_op jit(solution)/shard_map/dot_general | solution.py:15
  336.5 11.7 reduce-scatter.9.cloned.1.call-start
  348.3 21.9 %convolution_bitcast_fusion.1 = f32[3072,512]{0,1:T(8,128)} fusion(bf16[1536,512]{1,0:T(8,128)(2,1)S(1)} %copy-done.25, f32[3072,1536]{1,0:T(8,128)} %param.5), kind=kOutput, calls=%fused_computation.2 | convolution fusion | flops 28991029248 | bytes 26738688 | tf_op jit(solution)/shard_map/dot_general | solution.py:15
  370.2 61.4 %reduce-scatter.11.cloned.1.call-done = f32[384,512]{0,1:T(8,128)} async-done(((f32[3072,512]{0,1:T(8,128)}), f32[384,512]{0,1:T(8,128)}) %reduce-scatter.11.cloned.1.call-update) | async-done | bytes 786448 | tf_op jit(solution)/shard_map/reduce_scatter | solution.py:47
  431.6 120.7 %reduce-scatter.7.cloned.1.call-done = f32[384,512]{0,1:T(8,128)} async-done(((f32[3072,512]{0,1:T(8,128)}), f32[384,512]{0,1:T(8,128)}) %reduce-scatter.7.cloned.1.call-update) | async-done | bytes 786448 | tf_op jit(solution)/shard_map/reduce_scatter | solution.py:47
  552.4 4.1 convolution_add_fusion.4
  556.5 116.8 %reduce-scatter.9.cloned.1.call-done = f32[384,512]{0,1:T(8,128)} async-done(((f32[3072,512]{0,1:T(8,128)}), f32[384,512]{0,1:T(8,128)}) %reduce-scatter.9.cloned.1.call-update) | async-done | bytes 786448 | tf_op jit(solution)/shard_map/reduce_scatter | solution.py:47
  673.3 3.3 fusion.14
  676.7 1.9 fusion.15
  678.6 1.0 fusion.73
  679.5 3.1 fusion.6
  682.7 4.5 fusion
  687.1 2.1 fusion.64
  689.3 0.4 reduce-scatter.17.cloned.1.call-start
  689.7 20.7 %convolution_bitcast_fusion.3 = f32[1536,512]{0,1:T(8,128)} fusion(bf16[3072,512]{1,0:T(8,128)(2,1)} %all-gather.8.cloned.1.call-done, f32[3072,1536]{1,0:T(8,128)} %param.5), kind=kOutput, calls=%fused_computation.4 | convolution fusion | flops 28991029248 | bytes 25165824 | tf_op jit(solution)/shard_map/dot_general | solution.py:19
  710.5 20.8 %convolution_bitcast_fusion.5 = f32[1536,512]{0,1:T(8,128)} fusion(bf16[3072,512]{1,0:T(8,128)(2,1)} %all-gather.4.cloned.1.call-done, f32[3072,1536]{1,0:T(8,128)} %param.5), kind=kOutput, calls=%fused_computation.6 | convolution fusion | flops 28991029248 | bytes 25165824 | tf_op jit(solution)/shard_map/dot_general | solution.py:19
  731.3 0.2 reduce-scatter.15.cloned.1.call-start
  731.5 20.7 %convolution_bitcast_fusion.4 = f32[1536,512]{0,1:T(8,128)} fusion(bf16[3072,512]{1,0:T(8,128)(2,1)} %all-gather.6.cloned.1.call-done, f32[3072,1536]{1,0:T(8,128)} %param.5), kind=kOutput, calls=%fused_computation.5 | convolution fusion | flops 28991029248 | bytes 25165824 | tf_op jit(solution)/shard_map/dot_general | solution.py:19
  752.3 56.0 %all-reduce.9.cloned.1.call-done = (f32[512,1536]{1,0:T(8,128)}, f32[512,512]{1,0:T(8,128)}, f32[512,1024]{0,1:T(8,128)}) async-done(((f32[512,1536]{1,0:T(8,128)}, f32[512,512]{1,0:T(8,128)}, f32[512,1024]{0,1:T(8,128)}), (f32[512,1536]{1,0:T(8,128)}, f32[512,512]{1,0:T(8,128)}, f32[512,1024]{0,1:T(8,128)})) %all-reduce.9.cloned.1.call-update) | async-done | bytes 6291472 | tf_op jit(solution)/shard_map/psum | solution.py:58
  808.3 2.3 slice.74
  810.6 2.5 copy.65
  813.1 36.2 %reduce-scatter.17.cloned.1.call-done = f32[384,512]{0,1:T(8,128)} async-done(((f32[1536,512]{0,1:T(8,128)}), f32[384,512]{0,1:T(8,128)}) %reduce-scatter.17.cloned.1.call-update) | async-done | bytes 786448 | tf_op jit(solution)/shard_map/reduce_scatter | solution.py:78
  849.4 40.1 %reduce-scatter.13.cloned.1.call-done = f32[384,512]{0,1:T(8,128)} async-done(((f32[1536,512]{0,1:T(8,128)}), f32[384,512]{0,1:T(8,128)}) %reduce-scatter.13.cloned.1.call-update) | async-done | bytes 786448 | tf_op jit(solution)/shard_map/reduce_scatter | solution.py:78
  889.5 4.1 convolution_add_fusion.1
  893.6 36.2 %reduce-scatter.15.cloned.1.call-done = f32[384,512]{0,1:T(8,128)} async-done(((f32[1536,512]{0,1:T(8,128)}), f32[384,512]{0,1:T(8,128)}) %reduce-scatter.15.cloned.1.call-update) | async-done | bytes 786448 | tf_op jit(solution)/shard_map/reduce_scatter | solution.py:78
  929.8 3.4 fusion.16
  933.2 1.9 fusion.18
  935.2 1.6 pad_maximum_fusion.2
  936.7 3.1 copy.51
  939.8 3.2 pad_maximum_fusion.1
  943.0 3.2 copy.50
  946.3 198.1 %all-reduce.7.cloned.1.call-done = (f32[512,1536]{1,0:T(8,128)}, f32[512,512]{1,0:T(8,128)}, f32[512,1024]{0,1:T(8,128)}) async-done(((f32[512,1536]{1,0:T(8,128)}, f32[512,512]{1,0:T(8,128)}, f32[512,1024]{0,1:T(8,128)}), (f32[512,1536]{1,0:T(8,128)}, f32[512,512]{1,0:T(8,128)}, f32[512,1024]{0,1:T(8,128)})) %all-reduce.7.cloned.1.call-update) | async-done | bytes 6291472 | tf_op jit(solution)/shard_map/psum | solution.py:58
  1144.3 3.6 fusion.34
  1148.0 3.2 bitcast_subtract_fusion.7
  1151.2 1.9 fusion.32
  1153.1 1.9 fusion.27
  1155.0 2.0 fusion.13
  1157.0 1.0 copy-done.8
  1158.0 1.9 fusion.25
  1159.9 3.3 fusion.12
  1163.2 2.3 fusion.20
  1165.5 2.3 fusion.70
  1167.8 2.6 copy.39
  1170.4 5.3 fusion.11
  1175.7 2.0 maximum_bitcast_fusion.1
  1177.7 2.4 copy.49
  1180.1 2.3 maximum_bitcast_fusion.2
  1182.4 0.1 copy-done.17
  1182.5 0.3 copy-done.18
  1182.9 0.3 maximum_bitcast_fusion
  1183.2 5.1 pad_maximum_fusion
  (72 shorter events, 0.8 us)
Async XLA Ops:
  7.2 66.3 %all-gather.8.cloned.1.call-start = ((), (), s32[]{:S(2)}) async-start(), calls=%async_computation.10 | async-start | bytes 3538944 | tf_op jit(solution)/shard_map/all_gather | solution.py:43
  10.6 123.8 %all-gather.4.cloned.1.call-start = ((), (), s32[]{:S(2)}) async-start(), calls=%async_computation.6 | async-start | bytes 3538944 | tf_op jit(solution)/shard_map/all_gather | solution.py:43
  11.4 183.9 %all-gather.6.cloned.1.call-start = ((), (), s32[]{:S(2)}) async-start(), calls=%async_computation.8 | async-start | bytes 3538944 | tf_op jit(solution)/shard_map/all_gather | solution.py:43
  12.1 278.9 %all-reduce.11.cloned.1.call-start = ((), (), s32[]{:S(2)}) async-start(), calls=%async_computation.17 | async-start | bytes 9437184 | tf_op jit(solution)/shard_map/psum | solution.py:11
  198.2 233.5 %reduce-scatter.11.cloned.1.call-start = ((), (), s32[]{:S(2)}) async-start(), calls=%async_computation.11 | async-start | bytes 7077888 | tf_op jit(solution)/shard_map/reduce_scatter | solution.py:47
  313.3 1.4 copy-start.26
  313.3 239.1 %reduce-scatter.7.cloned.1.call-start = ((), (), s32[]{:S(2)}) async-start(), calls=%async_computation.7 | async-start | bytes 7077888 | tf_op jit(solution)/shard_map/reduce_scatter | solution.py:47
  336.5 11.7 copy-start.25
  336.5 336.7 %reduce-scatter.9.cloned.1.call-start = ((), (), s32[]{:S(2)}) async-start(), calls=%async_computation.9 | async-start | bytes 7077888 | tf_op jit(solution)/shard_map/reduce_scatter | solution.py:47
  370.2 182.2 %copy-start = (f32[3,512,512]{2,1,0:T(8,128)S(1)}, f32[3,512,512]{2,1,0:T(8,128)}, u32[]{:S(2)}) copy-start(f32[3,512,512]{2,1,0:T(8,128)} %param.7) | copy-start | bytes 9437188
  370.2 438.1 %all-reduce.9.cloned.1.call-start = ((), (), s32[]{:S(2)}) async-start(), calls=%async_computation.16 | async-start | bytes 12582912 | tf_op jit(solution)/shard_map/psum | solution.py:58
  673.3 3.4 copy-start.23
  673.3 5.3 copy-start.7
  676.6 6.0 copy-start.3
  676.6 2.9 copy-start.22
  678.5 4.1 copy-start.12
  678.5 4.1 copy-start.14
  682.7 4.5 copy-start.21
  689.3 160.1 %reduce-scatter.17.cloned.1.call-start = ((), (), s32[]{:S(2)}) async-start(), calls=%async_computation.14 | async-start | bytes 3932160 | tf_op jit(solution)/shard_map/reduce_scatter | solution.py:78
  710.4 179.1 %reduce-scatter.13.cloned.1.call-start = ((), (), s32[]{:S(2)}) async-start(), calls=%async_computation.12 | async-start | bytes 3932160 | tf_op jit(solution)/shard_map/reduce_scatter | solution.py:78
  731.3 198.5 %reduce-scatter.15.cloned.1.call-start = ((), (), s32[]{:S(2)}) async-start(), calls=%async_computation.13 | async-start | bytes 3932160 | tf_op jit(solution)/shard_map/reduce_scatter | solution.py:78
  752.2 392.1 %all-reduce.7.cloned.1.call-start = ((), (), s32[]{:S(2)}) async-start(), calls=%async_computation.15 | async-start | bytes 12582912 | tf_op jit(solution)/shard_map/psum | solution.py:58
  929.8 3.4 copy-start.24
  929.8 5.3 copy-start.13
  1144.3 3.6 copy-start.10
  1144.3 3.6 copy-start.11
  1151.1 3.8 copy-start.1
  1151.1 3.8 copy-start.15
  1151.1 3.8 copy-start.16
  1153.1 12.4 %copy-start.4 = (f32[512,512]{0,1:T(8,128)}, f32[512,512]{0,1:T(8,128)S(1)}, u32[]{:S(2)}) copy-start(f32[512,512]{0,1:T(8,128)S(1)} %fusion.32) | copy-start | bytes 3145732
  1155.0 4.9 copy-start.6
  1157.0 1.0 copy-start.8
  1159.9 5.6 copy-start.5
  1170.4 5.3 copy-start.9
  1170.4 5.3 copy-start.19
  1170.4 5.3 copy-start.20
  1180.0 2.4 copy-start.2
  1180.1 2.5 copy-start.17
  1180.1 2.8 copy-start.18
Sparse Core Ops, SparseCore 0:
  10.7 62.7 all-gather.7
  75.7 58.6 all-gather.3
  136.6 58.6 all-gather.5
  198.3 92.7 all-reduce.10
  313.4 118.1 reduce-scatter.10
  435.1 117.2 reduce-scatter.6
  556.0 117.2 reduce-scatter.8
  689.4 118.8 all-reduce.8
  811.4 37.9 reduce-scatter.16
  851.7 37.7 reduce-scatter.12
  892.0 37.7 reduce-scatter.14
  933.9 210.3 all-reduce.6
